TPU v7x, 32 devices: a whole 2x2x4 slice. The times are simulated.
32 devices in a mesh: band: 4 (over x, core), mem: 8 (over z, y).
Axes of the slice: x: 2, y: 2, z: 4, core: 2. Of those that a mesh axis runs over, the one named last changes fastest.
Arguments:
- members: bfloat16 [64, 16, 8192], P('band', None, 'mem'), may hold values from -6 to 6
- eigvecs: bfloat16 [112, 16, 8192], P('band', None, 'mem'), may hold values from -6 to 6
- control: float32 [112, 64], replicated, may hold values from -6 to 6
- columns: int32 [512, 16], P('mem'), may hold values from 0 to 1023
- interpolation: bfloat16 [512, 256, 512], P('mem'), may hold values from -0.375 to 0.375
- owners: int32 [512], replicated, may hold values from 0 to 7, as said below
- innovation: float32 [8, 256, 512], P('mem'), may hold values from -6 to 6
- obs_weight: float32 [8, 256, 512], P('mem'), may hold values from 0.25 to 4
Outputs:
- gradient: float32 [112, 64], P(None, 'band')
- departures: float32 [8, 256, 512], P('mem', None, 'band')
Inputs may be any that keep to these rules, and one draw needn't show every extreme that they name: `owners`: one tile sends at most 32 of its blocks to one owner, and some owner holds exactly 32 blocks from every tile.
All inputs are finite; a program needn't handle non-finite values.
Results may differ from a plain program's by a relative error of at most 0.0032.
Values may be sent and summed in bfloat16 or wider, within the bound.
A program may use at most 64 MiB of HBM per device.

v0:
```python
import math

import jax
import jax.numpy as jnp
from jax import lax
from jax.sharding import PartitionSpec as P


def per_device(members, eigvecs, control, columns, interpolation, owners, innovation, obs_weight):
    nband = lax.axis_size("band")
    tiles = lax.axis_size("mem")
    band_idx = lax.axis_index("band")
    tile_idx = lax.axis_index("mem")
    mem_dev, levels, tile_cols = members.shape
    blocks, patch = columns.shape
    obs_block = interpolation.shape[2]
    capacity = innovation.shape[1] // tiles
    modes, total_members = control.shape
    scale = 1.0 / math.sqrt(modes * total_members)
    control_b = control.astype(jnp.bfloat16)
    contract_first = (((0,), (0,)), ((), ()))
    contract_second = (((1,), (1,)), ((), ()))
    all_modes = lax.all_gather(eigvecs, "band", axis=0, tiled=True).reshape(modes, -1)
    weight_cols = lax.dynamic_slice_in_dim(control_b, band_idx * mem_dev, mem_dev, 1)
    mixed = lax.dot_general(
        weight_cols, all_modes, contract_first, preferred_element_type=jnp.float32
    )
    partial_field = scale * jnp.sum(members.reshape(mem_dev, -1) * mixed, axis=0)
    increment = lax.psum(partial_field, "band")
    increment_b = increment.reshape(levels, tile_cols).astype(jnp.bfloat16)
    picked = jnp.take(increment_b, columns.reshape(-1), axis=1).reshape(levels, blocks, patch)
    picked = jnp.transpose(picked, (1, 0, 2)).reshape(blocks, levels * patch)
    quarter = obs_block // nband
    innov_part = innovation[0]
    weight_part = obs_weight[0]
    image = jnp.einsum("jr,jro->jo", picked, interpolation, preferred_element_type=jnp.float32)
    local_owner = lax.dynamic_slice_in_dim(owners, tile_idx * blocks, blocks, 0)
    order = jnp.arange(blocks, dtype=jnp.int32)
    earlier = order[None, :] < order[:, None]
    same = local_owner[:, None] == local_owner[None, :]
    rank = jnp.sum(jnp.logical_and(same, earlier), axis=1)
    target = local_owner * capacity + rank
    placing = jnp.arange(tiles * capacity, dtype=jnp.int32)[:, None] == target[None, :]
    send = jnp.dot(placing.astype(jnp.float32), image, precision=lax.Precision.HIGHEST)
    arrived = lax.all_to_all(
        send.reshape(tiles, capacity, obs_block), "mem", split_axis=0, concat_axis=0, tiled=True
    )
    arrived = arrived.reshape(tiles * capacity, obs_block)
    counts = jnp.sum(owners.reshape(tiles, blocks) == tile_idx, axis=1)
    live = (jnp.arange(capacity)[None, :] < counts[:, None]).reshape(-1).astype(jnp.float32)
    departure = live[:, None] * weight_part * (innov_part - arrived)
    departure_b = departure.astype(jnp.bfloat16).reshape(tiles, capacity, obs_block)
    returned = lax.all_to_all(departure_b, "mem", split_axis=0, concat_axis=0, tiled=True).reshape(
        tiles * capacity, obs_block
    )
    own_back = jnp.dot(
        placing.T.astype(jnp.bfloat16), returned, preferred_element_type=jnp.float32
    ).astype(jnp.bfloat16)
    spread = jnp.einsum("jro,jo->jr", interpolation, own_back, preferred_element_type=jnp.float32)
    spread = jnp.transpose(spread.reshape(blocks, levels, patch), (1, 0, 2)).reshape(
        levels, blocks * patch
    )
    selector = (
        columns.reshape(-1)[:, None] == jnp.arange(tile_cols, dtype=jnp.int32)[None, :]
    ).astype(jnp.float32)
    adjoint = jnp.dot(spread, selector, precision=lax.Precision.HIGHEST)
    out_departure = lax.dynamic_slice_in_dim(departure, band_idx * quarter, quarter, 1)
    adjoint_flat = adjoint.reshape(-1)
    weighted = (members.reshape(mem_dev, -1) * adjoint_flat).astype(jnp.bfloat16)
    local_grad = lax.dot_general(
        all_modes, weighted, contract_second, preferred_element_type=jnp.float32
    )
    summed = lax.psum(local_grad, "mem")
    own_control = lax.dynamic_slice_in_dim(control, band_idx * mem_dev, mem_dev, 1)
    gradient = own_control - scale * summed
    return (gradient, out_departure[None])


def solution(mesh):
    return jax.shard_map(
        per_device,
        mesh=mesh,
        in_specs=(
            P("band", None, "mem"),
            P("band", None, "mem"),
            P(),
            P("mem", None),
            P("mem", None, None),
            P(),
            P("mem", None, None),
            P("mem", None, None),
        ),
        out_specs=(P(None, "band"), P("mem", None, "band")),
        check_vma=False,
    )
```

profile of v0, /device:TPU:0, one launch (start us, length us, event | category | flops | bytes accessed | tf_op | source)
XLA Modules:
  0.0 154.6 jit_solution(11151997983067209056)
XLA Ops:
  7.2 0.0 all-gather.2.cloned.1.call-start
  7.2 0.7 all-gather.2.cloned.1.call-update
  7.9 1.4 copy.39
  9.3 0.8 copy.28
  10.0 0.1 reshape.118
  10.1 0.8 dynamic_slice.13
  10.9 0.2 convert_reduce_fusion
  11.1 0.8 multiply_add_fusion
  11.8 0.7 compare_and_fusion
  12.6 31.2 %all-gather.2.cloned.1.call-done = bf16[112,16,1024]{2,1,0:T(8,128)(2,1)} async-done(((bf16[28,16,1024]{2,1,0:T(8,128)(2,1)}), bf16[112,16,1024]{2,1,0:T(8,128)(2,1)}) %all-gather.2.cloned.1.call-update) | async-done | bytes 3670032 | tf_op jit(solution)/shard_map/all_gather | solution.py:23
  43.8 4.4 %copy.40 = bf16[14,8,16,1024]{3,1,2,0:T(8,128)(2,1)S(1)} copy(bf16[14,8,16,1024]{3,2,1,0:T(8,128)(2,1)} %bitcast.45) | data formatting | bytes 7340032
  48.2 1.3 fusion.4
  49.5 10.8 %psum.14 = bf16[16384]{0:T(1024)(128)(2,1)S(1)} all-reduce(f32[16384]{0:T(1024)S(1)} %broadcast_multiply_fusion), channel_id=1, replica_groups=mesh['band'=4,'mem'=8] {'band'}, use_global_device_ids=true, to_apply=%region_3.4 | all-reduce | flops 16384 | bytes 98304 | tf_op jit(solution)/shard_map/psum | solution.py:29
  60.4 0.2 copy.29
  60.6 3.2 %gather_fusion = bf16[1024,16]{1,0:T(8,128)(2,1)S(1)} fusion(bf16[16,1024]{0,1:T(8,128)(2,1)S(1)} %copy.29, s32[1024]{0:T(1024)S(1)} %broadcast_clamp_fusion), kind=kCustom, calls=%fused_computation | custom fusion | bytes 69632 | tf_op jit(solution)/shard_map/jit(_take)/gather | solution.py:31
  63.8 0.3 copy.30
  64.1 0.1 copy.35
  64.2 0.0 copy-start.3
  64.2 0.0 copy-start.1
  64.2 0.0 copy-start.2
  64.2 8.1 %fusion.22 = f32[64,1,512]{2,1,0:T(1,128)S(1)} fusion(bf16[64,256,1]{1,2,0:T(2,128)(2,1)S(1)} %copy.35, bf16[64,256,512]{2,1,0:T(8,128)(2,1)} %param.12), kind=kOutput, calls=%fused_computation.42 | convolution fusion | flops 16777216 | bytes 16941056 | tf_op jit(solution)/shard_map/jr,jro->jo/dot_general | solution.py:36
  72.4 1.2 fusion.12
  73.6 5.7 %all-to-all-start = ((f32[8,32,512]{2,1,0:T(8,128)}), f32[8,32,512]{2,1,0:T(8,128)S(1)}, u32[]{:S(2)}, u32[]{:S(2)}) async-start(f32[8,32,512]{2,1,0:T(8,128)} %bitcast.9), calls=%async_computation | async-start | bytes 1048576 | tf_op jit(solution)/shard_map/all_to_all | solution.py:45
  79.3 0.0 copy-done.3
  79.3 0.1 reshape.126
  79.4 0.1 reduce_sum.28
  79.5 0.1 fusion.20
  79.6 14.5 %all-to-all-done = f32[8,32,512]{2,1,0:T(8,128)S(1)} async-done(((f32[8,32,512]{2,1,0:T(8,128)}), f32[8,32,512]{2,1,0:T(8,128)S(1)}, u32[]{:S(2)}, u32[]{:S(2)}) %all-to-all-start) | async-done | bytes 524320 | tf_op jit(solution)/shard_map/all_to_all | solution.py:45
  94.0 0.0 copy-done.1
  94.0 0.0 copy-done.2
  94.0 0.8 multiply_convert_fusion.1
  94.9 3.6 %all-to-all-start.1 = ((bf16[8,32,512]{2,1,0:T(8,128)(2,1)}), bf16[8,32,512]{2,1,0:T(8,128)(2,1)S(1)}, u32[]{:S(2)}, u32[]{:S(2)}) async-start(bf16[8,32,512]{2,1,0:T(8,128)(2,1)} %multiply_convert_fusion.1), calls=%async_computation.1 | async-start | bytes 524288 | tf_op jit(solution)/shard_map/all_to_all | solution.py:53
  98.5 0.1 reshape.124
  98.6 0.1 reshape.128
  98.7 0.8 fusion.11
  99.4 8.2 %all-to-all-done.1 = bf16[8,32,512]{2,1,0:T(8,128)(2,1)S(1)} async-done(((bf16[8,32,512]{2,1,0:T(8,128)(2,1)}), bf16[8,32,512]{2,1,0:T(8,128)(2,1)S(1)}, u32[]{:S(2)}, u32[]{:S(2)}) %all-to-all-start.1) | async-done | bytes 262176 | tf_op jit(solution)/shard_map/all_to_all | solution.py:53
  107.6 0.2 fusion.5
  107.8 0.0 copy-start
  107.8 10.2 %fusion.14 = f32[64,1,256]{2,1,0:T(1,128)S(1)} fusion(bf16[64,256,512]{2,1,0:T(8,128)(2,1)} %param.12, bf16[64,512,1]{1,0,2:T(8,128)(2,1)S(1)} %fusion.5), kind=kOutput, calls=%fused_computation.20 | convolution fusion | flops 16777216 | bytes 16908288 | tf_op jit(solution)/shard_map/jro,jo->jr/dot_general | solution.py:59
  118.1 0.1 copy.38
  118.2 0.2 copy.31
  118.4 0.3 reshape.123
  118.7 1.5 fusion
  120.1 0.0 copy-done
  120.1 0.1 multiply_convert_fusion
  120.3 6.5 %fusion.6 = f32[112,16]{0,1:T(8,128)S(1)} fusion(bf16[112,16,1024]{2,1,0:T(8,128)(2,1)} %all-gather.2.cloned.1.call-done, bf16[16,16,1024]{2,1,0:T(8,128)(2,1)S(1)} %multiply_convert_fusion), kind=kOutput, calls=%fused_computation.10 | convolution fusion | flops 58720256 | bytes 4201472 | tf_op jit(solution)/shard_map/dot_general | solution.py:70
  126.7 19.7 %psum.15 = f32[112,16]{0,1:T(8,128)S(1)} all-reduce(f32[112,16]{0,1:T(8,128)S(1)} %fusion.6), channel_id=1, replica_groups=mesh['band'=4,'mem'=8] {'mem'}, use_global_device_ids=true, to_apply=%region_4.5 | all-reduce | flops 1792 | bytes 14336 | tf_op jit(solution)/shard_map/psum | solution.py:73
  146.4 1.3 multiply_subtract_fusion
  (6 shorter events, 0.1 us)
Async XLA Ops:
  7.2 36.6 %all-gather.2.cloned.1.call-start = ((), (), s32[]{:S(2)}) async-start(), calls=%async_computation.2 | async-start | bytes 4587520 | tf_op jit(solution)/shard_map/all_gather | solution.py:23
  64.2 15.1 %copy-start.3 = (s32[512]{0:T(512)S(1)}, s32[512]{0:T(512)}, u32[]{:S(2)}) copy-start(s32[512]{0:T(512)} %param.13) | copy-start | bytes 6148
  64.2 29.8 %copy-start.1 = (f32[1,256,512]{2,1,0:T(8,128)S(1)}, f32[1,256,512]{2,1,0:T(8,128)}, u32[]{:S(2)}) copy-start(f32[1,256,512]{2,1,0:T(8,128)} %param.14) | copy-start | bytes 1572868
  64.2 29.8 %copy-start.2 = (f32[1,256,512]{2,1,0:T(8,128)S(1)}, f32[1,256,512]{2,1,0:T(8,128)}, u32[]{:S(2)}) copy-start(f32[1,256,512]{2,1,0:T(8,128)} %param.15) | copy-start | bytes 1572868
  73.6 20.5 %all-to-all-start = ((f32[8,32,512]{2,1,0:T(8,128)}), f32[8,32,512]{2,1,0:T(8,128)S(1)}, u32[]{:S(2)}, u32[]{:S(2)}) async-start(f32[8,32,512]{2,1,0:T(8,128)} %bitcast.9), calls=%async_computation | async-start | bytes 1048576 | tf_op jit(solution)/shard_map/all_to_all | solution.py:45
  94.9 12.7 %all-to-all-start.1 = ((bf16[8,32,512]{2,1,0:T(8,128)(2,1)}), bf16[8,32,512]{2,1,0:T(8,128)(2,1)S(1)}, u32[]{:S(2)}, u32[]{:S(2)}) async-start(bf16[8,32,512]{2,1,0:T(8,128)(2,1)} %multiply_convert_fusion.1), calls=%async_computation.1 | async-start | bytes 524288 | tf_op jit(solution)/shard_map/all_to_all | solution.py:53
  107.8 12.3 %copy-start = (bf16[16,16,1024]{2,1,0:T(8,128)(2,1)S(1)}, bf16[16,16,1024]{2,1,0:T(8,128)(2,1)}, u32[]{:S(2)}) copy-start(bf16[16,16,1024]{2,1,0:T(8,128)(2,1)} %param.8) | copy-start | bytes 1572868
Sparse Core Ops, SparseCore 0:
  9.5 34.1 all-gather.1
where the time goes:
time: 155 us
  waiting for transfers between devices  54.5 us (35%)
  blocking collectives  30.5 us (20%)
  matrix products  29 us (19%)
  between operations  14.2 us (9%)
  local copies, waits for them, and re-layouts  12 us (8%)
  starting transfers between devices  9.39 us (6%)
  other arithmetic  4.9 us (3%)
    all_gather x1, waiting for transfers between devices, per_device(): lax.all_gather(eigvecs, 'band', axis=0, tiled=True).reshape(modes, -1)  31.2 us
    psum x1, blocking collectives, per_device(): summed = lax.psum(local_grad, 'mem')  19.7 us
    all_to_all x1, waiting for transfers between devices, per_device(): lax.all_to_all(send.reshape(tiles, capacity, obs_block), 'mem', split_axi...  14.5 us
    psum x1, blocking collectives, per_device(): increment = lax.psum(partial_field, 'band')  10.8 us
    dot_general x1, matrix products, per_device(): jnp.einsum('jro,jo->jr', interpolation, own_back, preferred_element_type=...  10.2 us
    all_to_all x1, waiting for transfers between devices, per_device(): lax.all_to_all(departure_b, 'mem', split_axis=0, concat_axis=0, tiled=True)  8.18 us
    dot_general x1, matrix products, per_device(): jnp.einsum('jr,jro->jo', picked, interpolation, preferred_element_type=jn...  8.12 us
    unnamed x11, local copies, waits for them, and re-layouts  6.54 us
  transfers between devices with their start and end apart: 3, of which 3 were waited for; matrix products, arithmetic and copies ran while one was open for 4% of the time, Pallas kernels for 0%

commit v1 on v0

v1 whole, which is shorter than its diff:
```python
import math

import jax
import jax.numpy as jnp
from jax import lax
from jax.sharding import PartitionSpec as P


def per_device(members, eigvecs, control, columns, interpolation, owners, innovation, obs_weight):
    nband = lax.axis_size("band")
    tiles = lax.axis_size("mem")
    band_idx = lax.axis_index("band")
    tile_idx = lax.axis_index("mem")
    mem_dev, levels, tile_cols = members.shape
    own_modes = eigvecs.shape[0]
    blocks, patch = columns.shape
    obs_block = interpolation.shape[2]
    capacity = innovation.shape[1] // tiles
    modes, total_members = control.shape
    scale = 1.0 / math.sqrt(modes * total_members)
    quarter = obs_block // nband
    eig_t = jnp.transpose(eigvecs, (1, 0, 2))
    all_members = lax.all_gather(jnp.transpose(members, (1, 0, 2)), "band", axis=1, tiled=True)
    weights = lax.dynamic_slice_in_dim(control, band_idx * own_modes, own_modes, 0)
    weights = jnp.broadcast_to(weights.astype(jnp.bfloat16)[None], (levels, own_modes, total_members))
    mixed = jnp.einsum("lkm,lkg->lmg", weights, eig_t, preferred_element_type=jnp.float32)
    partial_field = scale * jnp.sum(all_members * mixed, axis=1)
    increment_b = lax.psum(partial_field, "band").astype(jnp.bfloat16)
    selector = columns.reshape(-1)[:, None] == jnp.arange(tile_cols, dtype=jnp.int32)[None, :]
    picked = lax.dot_general(
        increment_b,
        selector.astype(jnp.bfloat16),
        (((1,), (1,)), ((), ())),
        preferred_element_type=jnp.float32,
    ).astype(jnp.bfloat16)
    picked = jnp.transpose(picked.reshape(levels, blocks, patch), (1, 0, 2)).reshape(
        blocks, levels * patch
    )
    interp = lax.dynamic_slice_in_dim(interpolation, band_idx * quarter, quarter, 2)
    innov_part = lax.dynamic_slice_in_dim(innovation[0], band_idx * quarter, quarter, 1)
    weight_part = lax.dynamic_slice_in_dim(obs_weight[0], band_idx * quarter, quarter, 1)
    image = jnp.einsum("jr,jro->jo", picked, interp, preferred_element_type=jnp.float32)
    local_owner = lax.dynamic_slice_in_dim(owners, tile_idx * blocks, blocks, 0)
    order = jnp.arange(blocks, dtype=jnp.int32)
    earlier = order[None, :] < order[:, None]
    same = local_owner[:, None] == local_owner[None, :]
    rank = jnp.sum(jnp.logical_and(same, earlier), axis=1)
    target = local_owner * capacity + rank
    placing = jnp.arange(tiles * capacity, dtype=jnp.int32)[:, None] == target[None, :]
    send = jnp.dot(placing.astype(jnp.float32), image, precision=lax.Precision.HIGHEST)
    arrived = lax.all_to_all(
        send.reshape(tiles, capacity, quarter), "mem", split_axis=0, concat_axis=0, tiled=True
    )
    arrived = arrived.reshape(tiles * capacity, quarter)
    counts = jnp.sum(owners.reshape(tiles, blocks) == tile_idx, axis=1)
    live = (jnp.arange(capacity)[None, :] < counts[:, None]).reshape(-1).astype(jnp.float32)
    departure = live[:, None] * weight_part * (innov_part - arrived)
    departure_b = departure.astype(jnp.bfloat16).reshape(tiles, capacity, quarter)
    returned = lax.all_to_all(departure_b, "mem", split_axis=0, concat_axis=0, tiled=True).reshape(
        tiles * capacity, quarter
    )
    own_back = jnp.dot(
        placing.T.astype(jnp.bfloat16), returned, preferred_element_type=jnp.float32
    ).astype(jnp.bfloat16)
    spread = jnp.einsum("jro,jo->jr", interp, own_back, preferred_element_type=jnp.float32)
    spread = jnp.transpose(spread.reshape(blocks, levels, patch), (1, 0, 2)).reshape(
        levels, blocks * patch
    )
    adjoint = jnp.dot(spread, selector.astype(jnp.float32), precision=lax.Precision.HIGHEST)
    adjoint = lax.psum(adjoint, "band")
    weighted = (all_members * adjoint[:, None, :]).astype(jnp.bfloat16)
    local_grad = jnp.einsum("lkg,lmg->km", eig_t, weighted, preferred_element_type=jnp.float32)
    turned = lax.all_to_all(local_grad, "band", split_axis=1, concat_axis=0, tiled=True)
    summed = lax.psum(turned, "mem")
    own_control = lax.dynamic_slice_in_dim(control, band_idx * mem_dev, mem_dev, 1)
    gradient = own_control - scale * summed
    return (gradient, departure[None])


def solution(mesh):
    return jax.shard_map(
        per_device,
        mesh=mesh,
        in_specs=(
            P("band", None, "mem"),
            P("band", None, "mem"),
            P(),
            P("mem", None),
            P("mem", None, None),
            P(),
            P("mem", None, None),
            P("mem", None, None),
        ),
        out_specs=(P(None, "band"), P("mem", None, "band")),
        check_vma=False,
    )
```

time: 155 us -> 159 us (1.026)
  matrix products: 29 us -> 16.3 us
  blocking collectives: 30.5 us -> 41.8 us
  waiting for transfers between devices: 54.5 us -> 61.7 us
  local copies, waits for them, and re-layouts: 12 us -> 9.68 us
    psum x0 -> x1, waiting for transfers between devices: none -> 29 us  [per_device(): adjoint = lax.psum(adjoint, 'band')]
    dot_general x5 -> x6, matrix products: 27.6 us -> 15.3 us  [the longest x1 3.37 us: per_device(): jnp.einsum('jro,jo->jr', interp, own_back, preferred_element_type=jnp.flo...]
    all_to_all x2, waiting for transfers between devices: 22.6 us -> 10.7 us  [the longest x1 6.92 us: per_device(): lax.all_to_all(send.reshape(tiles, capacity, quarter), 'mem', split_axis=...]
    all_to_all x0 -> x1, blocking collectives: none -> 9.32 us  [per_device(): lax.all_to_all(departure_b, 'mem', split_axis=0, concat_axis=0, tiled=True)]
    all_gather x1, waiting for transfers between devices: 31.2 us -> 21.9 us  [per_device(): lax.all_gather(jnp.transpose(members, (1, 0, 2)), 'band', axis=1, tiled=T...]
    gather x2 -> x0, local copies, waits for them, and re-layouts: 3.5 us -> none  [per_device(): jnp.take(increment_b, columns.reshape(-1), axis=1)]
    unnamed x11, local copies, waits for them, and re-layouts: 6.54 us -> 3.9 us
    psum x2, blocking collectives: 30.5 us -> 32.4 us  [the longest x1 21.6 us: per_device(): summed = lax.psum(turned, 'mem')]
  transfers between devices with their start and end apart: 3 -> 4, of which waited for: 3 -> 4; matrix products, arithmetic and copies ran while one was open for 4% -> 2% of each run, Pallas kernels for 0% -> 0%
where the time goes in v1:
time: 159 us; the launch traced here: 158 us
  waiting for transfers between devices  61.7 us (39%)
  blocking collectives  41.8 us (26%)
  matrix products  16.3 us (10%)
  between operations  14.2 us (9%)
  local copies, waits for them, and re-layouts  9.68 us (6%)
  starting transfers between devices  9.04 us (6%)
  other arithmetic  5.1 us (3%)
    psum x1, waiting for transfers between devices, per_device(): adjoint = lax.psum(adjoint, 'band')  29 us
    all_gather x1, waiting for transfers between devices, per_device(): lax.all_gather(jnp.transpose(members, (1, 0, 2)), 'band', axis=1, tiled=T...  21.9 us
    psum x1, blocking collectives, per_device(): summed = lax.psum(turned, 'mem')  21.6 us
    psum x1, blocking collectives, per_device(): increment_b = lax.psum(partial_field, 'band').astype(jnp.bfloat16)  10.8 us
    all_to_all x1, blocking collectives, per_device(): lax.all_to_all(departure_b, 'mem', split_axis=0, concat_axis=0, tiled=True)  9.32 us
    all_to_all x1, waiting for transfers between devices, per_device(): lax.all_to_all(send.reshape(tiles, capacity, quarter), 'mem', split_axis=...  6.92 us
    all_to_all x1, starting transfers between devices, per_device(): lax.all_to_all(send.reshape(tiles, capacity, quarter), 'mem', split_axis=...  5.72 us
    unnamed x11, local copies, waits for them, and re-layouts  3.9 us
  transfers between devices with their start and end apart: 4, of which 4 were waited for; matrix products, arithmetic and copies ran while one was open for 2% of the time, Pallas kernels for 0%

profile of v1, /device:TPU:0, one launch (start us, length us, event | category | flops | bytes accessed | tf_op | source)
XLA Modules:
  0.0 157.8 jit_solution(15759564053056569046)
XLA Ops:
  7.2 0.0 copy-start
  7.2 0.0 all-gather.2.cloned.1.call-start
  7.2 2.2 %copy.60 = bf16[16,16,1024]{2,0,1:T(8,128)(2,1)} copy(bf16[16,16,1024]{2,1,0:T(8,128)(2,1)} %param.8) | data formatting | bytes 1048576 | tf_op args[0]
  9.4 0.0 all-gather.2.cloned.1.call-update
  9.5 0.8 constant_dynamic-slice_fusion
  10.3 0.1 copy.52
  10.4 0.8 copy.42
  11.2 0.1 eq.56
  11.3 0.8 dynamic_slice.24
  12.0 0.2 convert_reduce_fusion
  12.2 0.8 multiply_add_fusion
  13.0 21.9 %all-gather.2.cloned.1.call-done = bf16[16,64,1024]{2,1,0:T(8,128)(2,1)} async-done(((bf16[16,16,1024]{2,1,0:T(8,128)(2,1)}), bf16[16,64,1024]{2,1,0:T(8,128)(2,1)}) %all-gather.2.cloned.1.call-update) | async-done | bytes 2097168 | tf_op jit(solution)/shard_map/all_gather | solution.py:23
  34.9 0.0 copy-done
  34.9 3.2 %fusion = f32[16,1024]{1,0:T(8,128)S(1)} fusion(bf16[16,64,1024]{2,1,0:T(8,128)(2,1)} %all-gather.2.cloned.1.call-done, bf16[16,28,1024]{2,0,1:T(8,128)(2,1)S(1)} %bitcast.43, bf16[28,64]{1,0:T(8,128)(2,1)S(1)} %copy.52), kind=kOutput, calls=%fused_computation.2 | convolution fusion | flops 61849600 | bytes 3083776 | tf_op jit(solution)/shard_map/lkm,lkg->lmg/dot_general | solution.py:26
  38.1 0.0 copy-start.2
  38.1 10.8 %psum.21 = bf16[16,1024]{1,0:T(8,128)(2,1)S(1)} all-reduce(f32[16,1024]{1,0:T(8,128)S(1)} %broadcast_multiply_fusion), channel_id=1, replica_groups=mesh['band'=4,'mem'=8] {'band'}, use_global_device_ids=true, to_apply=%region_3.0 | all-reduce | flops 16384 | bytes 98304 | tf_op jit(solution)/shard_map/psum | solution.py:28
  49.0 0.9 fusion.13
  49.9 0.2 reshape.74
  50.1 0.1 copy.43
  50.2 0.1 copy.48
  50.4 2.8 %fusion.6 = f32[64,1,128]{2,1,0:T(1,128)S(1)} fusion(bf16[64,256,1]{1,2,0:T(2,128)(2,1)S(1)} %copy.48, bf16[64,256,512]{2,1,0:T(8,128)(2,1)} %param.12, s32[]{:T(128)S(6)} %select_n.15), kind=kOutput, calls=%fused_computation.9 | convolution fusion | flops 4194304 | bytes 4259844 | tf_op jit(solution)/shard_map/jr,jro->jo/dot_general | solution.py:42
  53.2 0.9 fusion.21
  54.1 5.7 %all-to-all-start = ((f32[8,32,128]{2,1,0:T(8,128)}), f32[8,32,128]{2,1,0:T(8,128)S(1)}, u32[]{:S(2)}, u32[]{:S(2)}) async-start(f32[8,32,128]{2,1,0:T(8,128)} %bitcast.9), calls=%async_computation | async-start | bytes 262144 | tf_op jit(solution)/shard_map/all_to_all | solution.py:51
  59.8 0.0 all-reduce.2.cloned.1.call-start
  59.8 0.0 copy-done.2
  59.9 0.1 reshape.81
  59.9 0.1 reduce_sum.28
  60.0 0.1 fusion.28
  60.1 0.1 reshape.82
  60.2 6.9 %all-to-all-done = f32[8,32,128]{2,1,0:T(8,128)S(1)} async-done(((f32[8,32,128]{2,1,0:T(8,128)}), f32[8,32,128]{2,1,0:T(8,128)S(1)}, u32[]{:S(2)}, u32[]{:S(2)}) %all-to-all-start) | async-done | bytes 131104 | tf_op jit(solution)/shard_map/all_to_all | solution.py:51
  67.1 0.0 copy-start.1
  67.1 1.9 %fusion.20 = (f32[1,256,128]{2,1,0:T(8,128)}, f32[1,256,128]{2,1,0:T(8,128)S(1)}, f32[1,256,128]{2,1,0:T(8,128)S(1)}) fusion(f32[256]{0:T(256)S(1)} %reshape.82, f32[1,256,512]{2,1,0:T(8,128)} %param.15, s32[]{:T(128)S(6)} %select_n.15, f32[1,256,512]{2,1,0:T(8,128)} %param.14, f32[1,256,128]{2,1,0:T(8,128)S(1)} %bitcast.46), kind=kLoop, calls=%fused_computation.23 | loop fusion | flops 98304 | bytes 787460 | tf_op jit(solution)/shard_map/mul | solution.py:57
  69.0 0.1 multiply_convert_fusion
  69.1 9.3 %all_to_all.29 = bf16[8,32,128]{2,1,0:T(8,128)(2,1)S(1)} all-to-all(bf16[8,32,128]{2,1,0:T(8,128)(2,1)S(1)} %multiply_convert_fusion), channel_id=1, replica_groups=mesh['band'=4,'mem'=8] {'mem'}, dimensions={0} | all-to-all | bytes 131072 | tf_op jit(solution)/shard_map/all_to_all | solution.py:59
  78.4 0.2 fusion.14
  78.6 3.4 %fusion.4 = f32[64,1,256]{2,1,0:T(1,128)S(1)} fusion(bf16[64,256,512]{2,1,0:T(8,128)(2,1)} %param.12, s32[]{:T(128)S(6)} %select_n.15, bf16[64,128,1]{1,0,2:T(8,128)(2,1)S(1)} %fusion.14), kind=kOutput, calls=%fused_computation.7 | convolution fusion | flops 4194304 | bytes 4276228 | tf_op jit(solution)/shard_map/jro,jo->jr/dot_general | solution.py:65
  82.0 0.8 copy.51
  82.8 1.1 copy.44
  83.9 0.9 reshape.79
  84.8 2.9 %fusion.2 = f32[16,1024]{1,0:T(8,128)} fusion(f32[16,1024]{1,0:T(8,128)} %reshape.79, s32[1024]{0:T(1024)S(1)} %eq.56), kind=kOutput, calls=%fused_computation.5 | convolution fusion | flops 202375168 | bytes 135168 | tf_op jit(solution)/shard_map/dot_general | solution.py:69
  87.7 0.0 all-reduce.2.cloned.1.call-update
  87.7 29.0 %all-reduce.2.cloned.1.call-done = f32[16,1024]{1,0:T(8,128)} async-done(((f32[16,1024]{1,0:T(8,128)}), f32[16,1024]{1,0:T(8,128)}) %all-reduce.2.cloned.1.call-update) | async-done | bytes 65552 | tf_op jit(solution)/shard_map/psum | solution.py:70
  116.8 0.0 copy-done.1
  116.8 2.0 %fusion.15 = f32[28,64]{1,0:T(8,128)S(1)} fusion(bf16[16,64,1024]{2,1,0:T(8,128)(2,1)S(1)} %copy-done.1, f32[16,1024]{1,0:T(8,128)} %all-reduce.2.cloned.1.call-done, bf16[16,28,1024]{2,0,1:T(8,128)(2,1)S(1)} %bitcast.44), kind=kOutput, calls=%fused_computation.18 | convolution fusion | flops 61865984 | bytes 3087360 | tf_op jit(solution)/shard_map/lkg,lmg->km/dot_general | solution.py:72
  118.8 0.1 copy.46
  118.9 0.7 reshape.88
  119.6 3.2 %all-to-all-start.2 = ((f32[4,1,448]{2,1,0:T(1,128)}), f32[4,1,448]{2,1,0:T(1,128)S(1)}, u32[]{:S(2)}, u32[]{:S(2)}) async-start(f32[4,1,448]{2,1,0:T(1,128)} %reshape.88), calls=%async_computation.2 | async-start | bytes 16384 | tf_op jit(solution)/shard_map/all_to_all | solution.py:73
  122.9 3.8 %all-to-all-done.2 = f32[4,1,448]{2,1,0:T(1,128)S(1)} async-done(((f32[4,1,448]{2,1,0:T(1,128)}), f32[4,1,448]{2,1,0:T(1,128)S(1)}, u32[]{:S(2)}, u32[]{:S(2)}) %all-to-all-start.2) | async-done | bytes 7200 | tf_op jit(solution)/shard_map/all_to_all | solution.py:73
  126.7 0.5 broadcast.15
  127.2 0.7 reduce
  127.9 0.1 reshape.89
  128.0 0.1 all_to_all.25
  128.1 21.6 %psum.23 = f32[112,16]{0,1:T(8,128)S(1)} all-reduce(f32[112,16]{0,1:T(8,128)S(1)} %all_to_all.25), channel_id=1, replica_groups=mesh['band'=4,'mem'=8] {'mem'}, use_global_device_ids=true, to_apply=%region_5.0 | all-reduce | flops 1792 | bytes 14336 | tf_op jit(solution)/shard_map/psum | solution.py:74
  149.7 1.3 multiply_subtract_fusion
  (4 shorter events, 0.0 us)
Async XLA Ops:
  7.2 27.7 %copy-start = (bf16[28,16,1024]{2,1,0:T(8,128)(2,1)S(1)}, bf16[28,16,1024]{2,1,0:T(8,128)(2,1)}, u32[]{:S(2)}) copy-start(bf16[28,16,1024]{2,1,0:T(8,128)(2,1)} %param.9) | copy-start | bytes 2752516
  7.2 27.7 %all-gather.2.cloned.1.call-start = ((), (), s32[]{:S(2)}) async-start(), calls=%async_computation.3 | async-start | bytes 2621440 | tf_op jit(solution)/shard_map/all_gather | solution.py:23
  38.1 21.7 %copy-start.2 = (s32[512]{0:T(512)S(1)}, s32[512]{0:T(512)}, u32[]{:S(2)}) copy-start(s32[512]{0:T(512)} %param.13) | copy-start | bytes 6148
  54.1 13.1 %all-to-all-start = ((f32[8,32,128]{2,1,0:T(8,128)}), f32[8,32,128]{2,1,0:T(8,128)S(1)}, u32[]{:S(2)}, u32[]{:S(2)}) async-start(f32[8,32,128]{2,1,0:T(8,128)} %bitcast.9), calls=%async_computation | async-start | bytes 262144 | tf_op jit(solution)/shard_map/all_to_all | solution.py:51
  59.8 57.0 %all-reduce.2.cloned.1.call-start = ((), (), s32[]{:S(2)}) async-start(), calls=%async_computation.4 | async-start | bytes 131072 | tf_op jit(solution)/shard_map/psum | solution.py:70
  67.1 49.7 %copy-start.1 = (bf16[16,64,1024]{2,1,0:T(8,128)(2,1)S(1)}, bf16[16,64,1024]{2,1,0:T(8,128)(2,1)}, u32[]{:S(2)}) copy-start(bf16[16,64,1024]{2,1,0:T(8,128)(2,1)} %all-gather.2.cloned.1.call-done) | copy-start | bytes 6291460
  119.6 7.0 %all-to-all-start.2 = ((f32[4,1,448]{2,1,0:T(1,128)}), f32[4,1,448]{2,1,0:T(1,128)S(1)}, u32[]{:S(2)}, u32[]{:S(2)}) async-start(f32[4,1,448]{2,1,0:T(1,128)} %reshape.88), calls=%async_computation.2 | async-start | bytes 16384 | tf_op jit(solution)/shard_map/all_to_all | solution.py:73
Sparse Core Ops, SparseCore 0:
  9.6 25.2 all-gather.1
  87.9 28.8 all-reduce.1

commit v2 on v1

--- a/solution.py
+++ b/solution.py
@@ -1,9 +1,232 @@
+import functools
 import math
 
 import jax
 import jax.numpy as jnp
 from jax import lax
+from jax.experimental import pallas as pl
+from jax.experimental.pallas import tpu as pltpu
 from jax.sharding import PartitionSpec as P
+
+MESH = pl.DeviceIdType.MESH
+CHUNKS = 4
+VMEM = pl.BlockSpec(memory_space=pltpu.VMEM)
+
+
+def greet(axes):
+    barrier = pltpu.get_barrier_semaphore()
+    total = 0
+    for axis, size in axes:
+        me = lax.axis_index(axis)
+        for step in range(1, size):
+            pl.semaphore_signal(
+                barrier, inc=1, device_id={axis: lax.rem(me + step, size)}, device_id_type=MESH
+            )
+        total += size - 1
+    pl.semaphore_wait(barrier, total)
+
+
+def remote(src, dst, send, recv, axis, peer):
+    return pltpu.make_async_remote_copy(
+        src_ref=src, dst_ref=dst, send_sem=send, recv_sem=recv,
+        device_id={axis: peer}, device_id_type=MESH,
+    )
+
+
+def spread_part(parts, send, recv, index, rows, size):
+    me = lax.axis_index("band")
+    copies = []
+    for step in range(1, size):
+        block = parts.at[me, rows]
+        copy = remote(
+            block, block, send.at[index, step - 1], recv.at[index, step - 1],
+            "band", lax.rem(me + step, size),
+        )
+        copy.start()
+        copies.append(copy)
+    return copies
+
+
+def field_kernel(
+    nband, scale, mem_ref, eig_ref, weight_ref, all_ref, inc_ref, mixed, parts,
+    core_send, core_recv, far_send, far_recv, relay_send, relay_recv, part_send, part_recv, own_sem,
+):
+    me = lax.axis_index("band")
+    levels, mem_dev, _ = mem_ref.shape
+    each = levels // CHUNKS
+    partner = me + 1 - 2 * lax.rem(me, 2)
+    far = lax.rem(me + 2, nband)
+    far_partner = lax.rem(partner + 2, nband)
+
+    def place(band, rows):
+        return all_ref.at[rows, pl.ds(pl.multiple_of(band * mem_dev, mem_dev), mem_dev)]
+
+    greet((("band", nband),))
+    chunks = [pl.ds(c * each, each) for c in range(CHUNKS)]
+    far_copies = []
+    for c, rows in enumerate(chunks):
+        copy = remote(
+            mem_ref.at[rows], place(me, rows), far_send.at[c], far_recv.at[c], "band", far
+        )
+        copy.start()
+        far_copies.append(copy)
+    whole = pl.ds(0, levels)
+    core_copy = remote(mem_ref, place(me, whole), core_send, core_recv, "band", partner)
+    core_copy.start()
+    own_copy = pltpu.make_async_copy(mem_ref, place(me, whole), own_sem)
+    own_copy.start()
+
+    def mix(level, carry):
+        mixed[level] = jnp.dot(
+            weight_ref[...], eig_ref[level], preferred_element_type=jnp.float32
+        )
+        return carry
+
+    lax.fori_loop(0, levels, mix, 0)
+    own_copy.wait()
+    core_copy.wait()
+    relays = []
+
+    def relay(c):
+        far_copies[c].wait()
+        copy = remote(
+            place(far, chunks[c]), place(far, chunks[c]), relay_send.at[c], relay_recv.at[c],
+            "band", partner,
+        )
+        copy.start()
+        relays.append(copy)
+
+    sends = []
+    relay(0)
+    for c, rows in enumerate(chunks):
+        if c + 1 < CHUNKS:
+            relay(c + 1)
+        relays[c].wait()
+        for i in range(each):
+            level = c * each + i
+            parts[me, level : level + 1] = jnp.sum(
+                all_ref[level].astype(jnp.float32) * mixed[level], axis=0, keepdims=True
+            )
+        sends += spread_part(parts, part_send, part_recv, c, rows, nband)
+    for copy in sends:
+        copy.wait()
+    total = parts[0]
+    for band in range(1, nband):
+        total = total + parts[band]
+    inc_ref[...] = (scale * total).astype(inc_ref.dtype)
+
+
+def exchange_kernel(
+    tiles, send_ref, innov_ref, weight_ref, dep_ref, back_ref, arrived, rounded,
+    out_send, out_recv, back_send, back_recv,
+):
+    me = lax.axis_index("mem")
+    greet((("mem", tiles),))
+    outs, backs = [], []
+    for step in range(1, tiles):
+        peer = lax.rem(me + step, tiles)
+        copy = remote(
+            send_ref.at[peer], arrived.at[me], out_send.at[step - 1], out_recv.at[step - 1],
+            "mem", peer,
+        )
+        copy.start()
+        outs.append(copy)
+    own = weight_ref[me] * (innov_ref[me] - send_ref[me])
+    dep_ref[me] = own
+    back_ref[me] = own.astype(back_ref.dtype)
+    for step in range(1, tiles):
+        source = lax.rem(me + tiles - step, tiles)
+        outs[step - 1].wait_recv()
+        value = weight_ref[source] * (innov_ref[source] - arrived[source])
+        dep_ref[source] = value
+        rounded[source] = value.astype(rounded.dtype)
+        copy = remote(
+            rounded.at[source], back_ref.at[me], back_send.at[step - 1], back_recv.at[step - 1],
+            "mem", source,
+        )
+        copy.start()
+        backs.append(copy)
+    for copy in outs:
+        copy.wait_send()
+    for copy in backs:
+        copy.wait()
+
+
+def gradient_kernel(
+    nband, tiles, scale, adj_ref, all_ref, eig_ref, control_ref, grad_ref,
+    parts, local, turned, sums,
+    part_send, part_recv, turn_send, turn_recv, sum_send, sum_recv,
+):
+    band = lax.axis_index("band")
+    tile = lax.axis_index("mem")
+    levels = adj_ref.shape[0]
+    each = levels // CHUNKS
+    modes_dev = eig_ref.shape[1]
+    mem_dev = local.shape[1]
+    greet((("band", nband), ("mem", tiles)))
+    parts[band] = adj_ref[...]
+    sends = []
+    for c in range(CHUNKS):
+        sends.append(spread_part(parts, part_send, part_recv, c, pl.ds(c * each, each), nband))
+    local[...] = jnp.zeros_like(local)
+    total = None
+    for c in range(CHUNKS):
+        for copy in sends[c]:
+            copy.wait()
+        for i in range(each):
+            level = c * each + i
+            row = parts[0, level : level + 1]
+            for b in range(1, nband):
+                row = row + parts[b, level : level + 1]
+            weighted = (all_ref[level].astype(jnp.float32) * row).astype(jnp.bfloat16)
+            term = lax.dot_general(
+                weighted, eig_ref[level], (((1,), (1,)), ((), ())),
+                preferred_element_type=jnp.float32,
+            )
+            total = term if total is None else total + term
+    for b in range(nband):
+        local[b, :, :modes_dev] = total[b * mem_dev : (b + 1) * mem_dev]
+    copies = []
+    for step in range(1, nband):
+        peer = lax.rem(band + step, nband)
+        copy = remote(
+            local.at[peer], turned.at[band], turn_send.at[step - 1], turn_recv.at[step - 1],
+            "band", peer,
+        )
+        copy.start()
+        copies.append(copy)
+    turned[band] = local[band]
+    for copy in copies:
+        copy.wait()
+    own = turned[0]
+    for b in range(1, nband):
+        own = own + pltpu.roll(turned[b], b * modes_dev, 1)
+    sums[tile] = own
+    copies = []
+    for step in range(1, tiles):
+        peer = lax.rem(tile + step, tiles)
+        copy = remote(
+            sums.at[tile], sums.at[tile], sum_send.at[step - 1], sum_recv.at[step - 1],
+            "mem", peer,
+        )
+        copy.start()
+        copies.append(copy)
+    for copy in copies:
+        copy.wait()
+    whole = sums[0]
+    for t in range(1, tiles):
+        whole = whole + sums[t]
+    grad_ref[...] = control_ref[...] - scale * whole[:, : grad_ref.shape[1]]
+
+
+def dma(*shape):
+    return pltpu.SemaphoreType.DMA(shape)
+
+
+def params(collective_id):
+    return pltpu.CompilerParams(
+        collective_id=collective_id, has_side_effects=True, vmem_limit_bytes=40 << 20
+    )
 
 
 def per_device(members, eigvecs, control, columns, interpolation, owners, innovation, obs_weight):
@@ -20,12 +243,25 @@
     scale = 1.0 / math.sqrt(modes * total_members)
     quarter = obs_block // nband
     eig_t = jnp.transpose(eigvecs, (1, 0, 2))
-    all_members = lax.all_gather(jnp.transpose(members, (1, 0, 2)), "band", axis=1, tiled=True)
+    mem_t = jnp.transpose(members, (1, 0, 2))
     weights = lax.dynamic_slice_in_dim(control, band_idx * own_modes, own_modes, 0)
-    weights = jnp.broadcast_to(weights.astype(jnp.bfloat16)[None], (levels, own_modes, total_members))
-    mixed = jnp.einsum("lkm,lkg->lmg", weights, eig_t, preferred_element_type=jnp.float32)
-    partial_field = scale * jnp.sum(all_members * mixed, axis=1)
-    increment_b = lax.psum(partial_field, "band").astype(jnp.bfloat16)
+    weights = weights.astype(jnp.bfloat16).T
+    all_members, increment_b = pl.pallas_call(
+        functools.partial(field_kernel, nband, scale),
+        out_shape=(
+            jax.ShapeDtypeStruct((levels, total_members, tile_cols), jnp.bfloat16),
+            jax.ShapeDtypeStruct((levels, tile_cols), jnp.bfloat16),
+        ),
+        in_specs=[VMEM] * 3,
+        out_specs=(VMEM, VMEM),
+        scratch_shapes=[
+            pltpu.VMEM((levels, total_members, tile_cols), jnp.float32),
+            pltpu.VMEM((nband, levels, tile_cols), jnp.float32),
+            dma(), dma(), dma(CHUNKS), dma(CHUNKS), dma(CHUNKS), dma(CHUNKS),
+            dma(CHUNKS, nband - 1), dma(CHUNKS, nband - 1), dma(),
+        ],
+        compiler_params=params(1),
+    )(mem_t, eig_t, weights)
     selector = columns.reshape(-1)[:, None] == jnp.arange(tile_cols, dtype=jnp.int32)[None, :]
     picked = lax.dot_general(
         increment_b,
@@ -48,17 +284,26 @@
     target = local_owner * capacity + rank
     placing = jnp.arange(tiles * capacity, dtype=jnp.int32)[:, None] == target[None, :]
     send = jnp.dot(placing.astype(jnp.float32), image, precision=lax.Precision.HIGHEST)
-    arrived = lax.all_to_all(
-        send.reshape(tiles, capacity, quarter), "mem", split_axis=0, concat_axis=0, tiled=True
-    )
-    arrived = arrived.reshape(tiles * capacity, quarter)
     counts = jnp.sum(owners.reshape(tiles, blocks) == tile_idx, axis=1)
-    live = (jnp.arange(capacity)[None, :] < counts[:, None]).reshape(-1).astype(jnp.float32)
-    departure = live[:, None] * weight_part * (innov_part - arrived)
-    departure_b = departure.astype(jnp.bfloat16).reshape(tiles, capacity, quarter)
-    returned = lax.all_to_all(departure_b, "mem", split_axis=0, concat_axis=0, tiled=True).reshape(
-        tiles * capacity, quarter
-    )
+    live = (jnp.arange(capacity)[None, :] < counts[:, None]).astype(jnp.float32)
+    slots = (tiles, capacity, quarter)
+    live_weight = live[:, :, None] * weight_part.reshape(slots)
+    departure, returned = pl.pallas_call(
+        functools.partial(exchange_kernel, tiles),
+        out_shape=(
+            jax.ShapeDtypeStruct(slots, jnp.float32),
+            jax.ShapeDtypeStruct(slots, jnp.bfloat16),
+        ),
+        in_specs=[VMEM] * 3,
+        out_specs=(VMEM, VMEM),
+        scratch_shapes=[
+            pltpu.VMEM(slots, jnp.float32), pltpu.VMEM(slots, jnp.bfloat16),
+            dma(tiles - 1), dma(tiles - 1), dma(tiles - 1), dma(tiles - 1),
+        ],
+        compiler_params=params(2),
+    )(send.reshape(slots), innov_part.reshape(slots), live_weight)
+    departure = departure.reshape(tiles * capacity, quarter)
+    returned = returned.reshape(tiles * capacity, quarter)
     own_back = jnp.dot(
         placing.T.astype(jnp.bfloat16), returned, preferred_element_type=jnp.float32
     ).astype(jnp.bfloat16)
@@ -67,13 +312,23 @@
         levels, blocks * patch
     )
     adjoint = jnp.dot(spread, selector.astype(jnp.float32), precision=lax.Precision.HIGHEST)
-    adjoint = lax.psum(adjoint, "band")
-    weighted = (all_members * adjoint[:, None, :]).astype(jnp.bfloat16)
-    local_grad = jnp.einsum("lkg,lmg->km", eig_t, weighted, preferred_element_type=jnp.float32)
-    turned = lax.all_to_all(local_grad, "band", split_axis=1, concat_axis=0, tiled=True)
-    summed = lax.psum(turned, "mem")
     own_control = lax.dynamic_slice_in_dim(control, band_idx * mem_dev, mem_dev, 1)
-    gradient = own_control - scale * summed
+    lanes = pl.cdiv(modes, 128) * 128
+    gradient = pl.pallas_call(
+        functools.partial(gradient_kernel, nband, tiles, scale),
+        out_shape=jax.ShapeDtypeStruct((mem_dev, modes), jnp.float32),
+        in_specs=[VMEM] * 4,
+        out_specs=VMEM,
+        scratch_shapes=[
+            pltpu.VMEM((nband, levels, tile_cols), jnp.float32),
+            pltpu.VMEM((nband, mem_dev, lanes), jnp.float32),
+            pltpu.VMEM((nband, mem_dev, lanes), jnp.float32),
+            pltpu.VMEM((tiles, mem_dev, lanes), jnp.float32),
+            dma(CHUNKS, nband - 1), dma(CHUNKS, nband - 1),
+            dma(nband - 1), dma(nband - 1), dma(tiles - 1), dma(tiles - 1),
+        ],
+        compiler_params=params(3),
+    )(adjoint, all_members, eig_t, own_control.T).T
     return (gradient, departure[None])
 
 

time: 159 us -> 71.4 us (0.45)
  waiting for transfers between devices: 61.7 us -> 0 us
  Pallas kernels: 0 us -> 49.1 us
  blocking collectives: 41.8 us -> 0 us
  between operations: 14.2 us -> 0.78 us
  starting transfers between devices: 9.04 us -> 0 us
  matrix products: 16.3 us -> 9 us
  other arithmetic: 5.1 us -> 1.46 us
    pallas_call x0 -> x3, Pallas kernels: none -> 49.1 us  [the longest x1 21.1 us: per_device(): pl.pallas_call(functools.partial(field_kernel, nband, scale), out_shape=(...]
    psum x2 -> x0, blocking collectives: 32.4 us -> none  [the longest x1 21.6 us: per_device(): summed = lax.psum(turned, 'mem')]
    psum x1 -> x0, waiting for transfers between devices: 29 us -> none  [per_device(): adjoint = lax.psum(adjoint, 'band')]
    all_gather x1 -> x0, waiting for transfers between devices: 21.9 us -> none  [per_device(): lax.all_gather(jnp.transpose(members, (1, 0, 2)), 'band', axis=1, tiled=T...]
    all_to_all x2 -> x0, waiting for transfers between devices: 10.7 us -> none  [the longest x1 6.92 us: per_device(): lax.all_to_all(send.reshape(tiles, capacity, quarter), 'mem', split_axis=...]
    all_to_all x1 -> x0, blocking collectives: 9.32 us -> none  [per_device(): lax.all_to_all(departure_b, 'mem', split_axis=0, concat_axis=0, tiled=True)]
    all_to_all x2 -> x0, starting transfers between devices: 8.97 us -> none  [the longest x1 5.72 us: per_device(): lax.all_to_all(send.reshape(tiles, capacity, quarter), 'mem', split_axis=...]
    dot_general x2 -> x0, matrix products: 5.24 us -> none  [the longest x1 3.2 us: per_device(): jnp.einsum('lkm,lkg->lmg', weights, eig_t, preferred_element_type=jnp.flo...]
  transfers between devices with their start and end apart: 4 -> 0, of which waited for: 4 -> 0; matrix products, arithmetic and copies ran while one was open for 2% -> 0% of each run, Pallas kernels for 0% -> 0%
where the time goes in v2:
time: 71.4 us; the launch traced here: 71 us
  Pallas kernels  49.1 us (69%)
  local copies, waits for them, and re-layouts  10.6 us (15%)
  matrix products  9 us (13%)
  other arithmetic  1.46 us (2%)
  between operations  0.78 us (1%)
    pallas_call x1, Pallas kernels, per_device(): pl.pallas_call(functools.partial(field_kernel, nband, scale), out_shape=(...  21.1 us
    pallas_call x1, Pallas kernels, per_device(): pl.pallas_call(functools.partial(exchange_kernel, tiles), out_shape=(jax....  14.3 us
    pallas_call x1, Pallas kernels, per_device(): pl.pallas_call(functools.partial(gradient_kernel, nband, tiles, scale), o...  13.7 us
    unnamed x15, local copies, waits for them, and re-layouts  5.77 us
    dot_general x1, matrix products, per_device(): jnp.einsum('jro,jo->jr', interp, own_back, preferred_element_type=jnp.flo...  3.4 us
    dot_general x1, matrix products, per_device(): jnp.einsum('jr,jro->jo', picked, interp, preferred_element_type=jnp.float32)  2.84 us
    dynamic_slice x1, local copies, waits for them, and re-layouts, per_device(): lax.dynamic_slice_in_dim(obs_weight[0], band_idx * quarter, quarter, 1)  1.65 us
    dot_general x1, matrix products, per_device(): jnp.dot(spread, selector.astype(jnp.float32), precision=lax.Precision.HIG...  1.46 us

profile of v2, /device:TPU:0, one launch (start us, length us, event | category | flops | bytes accessed | tf_op | source)
XLA Modules:
  0.0 71.0 jit_solution(2929764192561235555)
XLA Ops:
  0.6 0.0 copy-start
  0.6 0.0 copy-start.3
  0.7 0.7 %copy-done = f32[112,64]{0,1:T(8,128)S(1)} copy-done((f32[112,64]{0,1:T(8,128)S(1)}, f32[112,64]{0,1:T(8,128)}, u32[]{:S(2)}) %copy-start) | copy-done | bytes 28696
  1.4 0.1 fusion.15.weight_ref
  1.5 1.7 %copy.30 = bf16[28,16,1024]{2,0,1:T(8,128)(2,1)S(1)} copy(bf16[28,16,1024]{2,1,0:T(8,128)(2,1)} %param.9) | data formatting | bytes 1835008 | tf_op args[1]
  3.2 1.3 %copy.31 = bf16[16,16,1024]{2,0,1:T(8,128)(2,1)S(1)} copy(bf16[16,16,1024]{2,1,0:T(8,128)(2,1)} %param.8) | data formatting | bytes 1048576 | tf_op args[0]
  4.5 0.0 copy-start.4
  4.5 21.1 %shard_map.95 = (bf16[16,64,1024]{2,1,0:T(8,128)(2,1)S(1)}, bf16[16,1024]{1,0:T(8,128)(2,1)S(1)}) custom-call(bf16[16,16,1024]{2,1,0:T(8,128)(2,1)S(1)} %bitcast.36, bf16[16,28,1024]{2,1,0:T(8,128)(2,1)S(1)} %bitcast.34, bf16[64,28]{1,0:T(8,128)(2,1)S(1)} %fusion.15.weight_ref), custom_call_target="tpu_custom_call" | custom-call | tf_op jit(solution)/shard_map/pallas_call | solution.py:249
  25.6 0.0 copy-done.3
  25.6 0.1 copy.19
  25.7 0.1 eq.54
  25.8 0.9 %fusion.8 = bf16[16,1024]{1,0:T(8,128)(2,1)S(1)} fusion(bf16[16,1024]{1,0:T(8,128)(2,1)S(1)} %get-tuple-element.6, s32[1024]{0:T(1024)S(1)} %eq.54), kind=kOutput, calls=%fused_computation.9 | convolution fusion | flops 34619392 | bytes 69632 | tf_op jit(solution)/shard_map/dot_general | solution.py:266
  26.7 0.2 reshape.63
  26.9 0.1 copy.20
  27.0 0.1 copy.22
  27.2 2.8 %fusion.4 = f32[64,1,128]{2,1,0:T(1,128)S(1)} fusion(bf16[64,256,1]{1,2,0:T(2,128)(2,1)S(1)} %copy.22, bf16[64,256,512]{2,1,0:T(8,128)(2,1)} %param.12, s32[]{:T(128)S(6)} %select_n.14), kind=kOutput, calls=%fused_computation.5 | convolution fusion | flops 4194304 | bytes 4259844 | tf_op jit(solution)/shard_map/jr,jro->jo/dot_general | solution.py:278
  30.0 0.0 copy-done.4
  30.0 0.1 dynamic_slice.19
  30.1 0.2 convert_reduce_fusion
  30.3 0.1 multiply_add_fusion
  30.4 0.2 fusion.10
  30.6 1.7 %constant_dynamic-slice_fusion = (f32[1,256,128]{2,1,0:T(8,128)}, f32[1,256,128]{2,1,0:T(8,128)S(1)}) fusion(f32[1,256,512]{2,1,0:T(8,128)} %param.15, s32[]{:T(128)S(6)} %select_n.14, f32[1,256,512]{2,1,0:T(8,128)} %param.14), kind=kLoop, calls=%fused_computation.30 | loop fusion | bytes 524292 | tf_op jit(solution)/shard_map/dynamic_slice | solution.py:277
  32.2 0.1 reshape.71
  32.3 0.1 reduce_sum.19
  32.4 0.1 fusion.16
  32.5 1.0 %broadcast_multiply_fusion.weight_ref = f32[8,32,128]{2,1,0:T(8,128)S(1)} fusion(f32[8,32,128]{2,1,0:T(8,128)} %bitcast.43, f32[8,32]{1,0:T(8,128)S(1)} %fusion.16), kind=kLoop, calls=%fused_computation.16 | loop fusion | flops 32768 | bytes 263168 | tf_op jit(solution)/shard_map/mul | solution.py:290
  33.5 14.3 %shard_map.96 = (f32[8,32,128]{2,1,0:T(8,128)S(1)}, bf16[8,32,128]{2,1,0:T(8,128)(2,1)S(1)}) custom-call(f32[8,32,128]{2,1,0:T(8,128)S(1)} %bitcast.37, f32[8,32,128]{2,1,0:T(8,128)S(1)} %bitcast.38, f32[8,32,128]{2,1,0:T(8,128)S(1)} %broadcast_multiply_fusion.weight_ref), custom_call_target="tpu_custom_call" | custom-call | tf_op jit(solution)/shard_map/pallas_call | solution.py:291
  47.8 0.0 copy-start.1
  47.8 0.6 copy-done.1
  48.4 0.2 fusion.9
  48.6 0.0 copy-start.2
  48.6 3.4 %fusion.2 = f32[64,1,256]{2,1,0:T(1,128)S(1)} fusion(bf16[64,256,512]{2,1,0:T(8,128)(2,1)} %param.12, s32[]{:T(128)S(6)} %select_n.14, bf16[64,128,1]{1,0,2:T(8,128)(2,1)S(1)} %fusion.9), kind=kOutput, calls=%fused_computation.3 | convolution fusion | flops 4194304 | bytes 4276228 | tf_op jit(solution)/shard_map/jro,jo->jr/dot_general | solution.py:310
  52.0 0.1 copy.25
  52.2 1.0 %copy.21 = f32[16,64,16]{2,1,0:T(8,128)} copy(f32[16,64,16]{1,2,0:T(8,128)S(1)} %bitcast.44) | data formatting | bytes 131072 | tf_op jit(solution)/shard_map/transpose | solution.py:311
  53.2 1.3 %reshape.70 = f32[16,1024]{1,0:T(8,128)S(1)} reshape(f32[16,64,16]{2,1,0:T(8,128)} %copy.21) | data formatting | bytes 131072 | tf_op jit(solution)/shard_map/reshape | solution.py:311
  54.5 1.5 %fusion.adj_ref = f32[16,1024]{1,0:T(8,128)S(1)} fusion(f32[16,1024]{1,0:T(8,128)S(1)} %reshape.70, s32[1024]{0:T(1024)S(1)} %eq.54), kind=kOutput, calls=%fused_computation.1 | convolution fusion | flops 202375168 | bytes 135168 | tf_op jit(solution)/shard_map/dot_general | solution.py:314
  56.0 13.7 %shard_map.97 = f32[16,112]{1,0:T(8,128)S(1)} custom-call(f32[16,1024]{1,0:T(8,128)S(1)} %fusion.adj_ref, bf16[16,64,1024]{2,1,0:T(8,128)(2,1)S(1)} %get-tuple-element.8.all_ref, bf16[16,28,1024]{2,1,0:T(8,128)(2,1)S(1)} %bitcast.35, f32[16,112]{1,0:T(8,128)S(1)} %dynamic-slice_bitcast_fusion.control_ref), custom_call_target="tpu_custom_call" | custom-call | tf_op jit(solution)/shard_map/pallas_call | solution.py:317
  69.7 0.6 copy.34
  70.3 0.0 copy-done.2
  70.3 0.7 copy.35
  (2 shorter events, 0.0 us)
Async XLA Ops:
  0.6 0.8 %copy-start = (f32[112,64]{0,1:T(8,128)S(1)}, f32[112,64]{0,1:T(8,128)}, u32[]{:S(2)}) copy-start(f32[112,64]{0,1:T(8,128)} %param.10) | copy-start | bytes 86020
  0.6 25.0 %copy-start.3 = (s32[64,16]{0,1:T(8,128)S(1)}, s32[64,16]{0,1:T(8,128)}, u32[]{:S(2)}) copy-start(s32[64,16]{0,1:T(8,128)} %param.11) | copy-start | bytes 12292
  4.5 25.5 %copy-start.4 = (s32[512]{0:T(512)S(1)}, s32[512]{0:T(512)}, u32[]{:S(2)}) copy-start(s32[512]{0:T(512)} %param.13) | copy-start | bytes 6148
  47.8 0.7 copy-start.1
  48.6 21.7 %copy-start.2 = (f32[8,32,128]{2,1,0:T(8,128)S(1)}, f32[8,32,128]{2,1,0:T(8,128)}, u32[]{:S(2)}) copy-start(f32[8,32,128]{2,1,0:T(8,128)} %copy-done.1) | copy-start | bytes 393220

commit v3 on v2

v3 whole, which is shorter than its diff:
```python
import functools
import math

import jax
import jax.numpy as jnp
from jax import lax
from jax.experimental import pallas as pl
from jax.experimental.pallas import tpu as pltpu
from jax.sharding import PartitionSpec as P

MESH = pl.DeviceIdType.MESH
CHUNKS = 4
VMEM = pl.BlockSpec(memory_space=pltpu.VMEM)


def greet(axes):
    barrier = pltpu.get_barrier_semaphore()
    total = 0
    for axis, size in axes:
        me = lax.axis_index(axis)
        for step in range(1, size):
            pl.semaphore_signal(
                barrier, inc=1, device_id={axis: lax.rem(me + step, size)}, device_id_type=MESH
            )
        total += size - 1
    pl.semaphore_wait(barrier, total)


def remote(src, dst, send, recv, axis, peer):
    return pltpu.make_async_remote_copy(
        src_ref=src, dst_ref=dst, send_sem=send, recv_sem=recv,
        device_id={axis: peer}, device_id_type=MESH,
    )


def spread_part(parts, send, recv, index, rows, size):
    me = lax.axis_index("band")
    copies = []
    for step in range(1, size):
        block = parts.at[me, rows]
        copy = remote(
            block, block, send.at[index, step - 1], recv.at[index, step - 1],
            "band", lax.rem(me + step, size),
        )
        copy.start()
        copies.append(copy)
    return copies


def split(value):
    high = value.astype(jnp.bfloat16)
    return high, (value - high.astype(jnp.float32)).astype(jnp.bfloat16)


def whole_kernel(
    nband, tiles, scale, mem_ref, eig_ref, weight_ref, cols_ref, target_ref, counts_ref,
    control_ref, interp_hbm, innov_hbm, obs_hbm, grad_ref, dep_ref,
    all_ref, mixed, parts, adj_parts, select, interp, innov, obs, image, spread, send, arrived,
    rounded, back, back_own, local, turned, sums,
    load_sem, core_send, core_recv, far_send, far_recv, relay_send, relay_recv,
    part_send, part_recv, out_send, out_recv, back_send, back_recv,
    adj_send, adj_recv, turn_send, turn_recv, sum_send, sum_recv,
):
    me = lax.axis_index("band")
    tile = lax.axis_index("mem")
    levels, mem_dev, tile_cols = mem_ref.shape
    modes_dev = eig_ref.shape[1]
    patch, blocks = cols_ref.shape
    capacity, quarter = send.shape[1:]
    each = levels // CHUNKS
    partner = me + 1 - 2 * lax.rem(me, 2)
    far = lax.rem(me + 2, nband)
    chunks = [pl.ds(c * each, each) for c in range(CHUNKS)]
    whole = pl.ds(0, levels)
    own_obs = pl.ds(pl.multiple_of(me * quarter, quarter), quarter)

    def place(band, rows):
        return all_ref.at[rows, pl.ds(pl.multiple_of(band * mem_dev, mem_dev), mem_dev)]

    own_copy = pltpu.make_async_copy(mem_ref, place(me, whole), load_sem.at[0])
    loads = [
        pltpu.make_async_copy(interp_hbm.at[:, :, own_obs], interp, load_sem.at[1]),
        pltpu.make_async_copy(innov_hbm.at[:, :, own_obs], innov, load_sem.at[2]),
        pltpu.make_async_copy(obs_hbm.at[:, :, own_obs], obs, load_sem.at[3]),
    ]
    greet((("band", nband), ("mem", tiles)))
    far_copies = []
    for c, rows in enumerate(chunks):
        copy = remote(
            mem_ref.at[rows], place(me, rows), far_send.at[c], far_recv.at[c], "band", far
        )
        copy.start()
        far_copies.append(copy)
    core_copy = remote(mem_ref, place(me, whole), core_send, core_recv, "band", partner)
    core_copy.start()
    own_copy.start()
    for copy in loads:
        copy.start()

    def mix(level, carry):
        mixed[level] = jnp.dot(
            weight_ref[...], eig_ref[level], preferred_element_type=jnp.float32
        )
        return carry

    lax.fori_loop(0, levels, mix, 0)
    column = lax.broadcasted_iota(jnp.int32, (patch, tile_cols), 1)
    for j in range(blocks):
        select[j * patch : (j + 1) * patch] = jnp.where(
            cols_ref[:, j : j + 1] == column, 1.0, 0.0
        ).astype(jnp.bfloat16)
    slot = lax.broadcasted_iota(jnp.int32, (tiles * capacity, blocks), 0)
    placing = jnp.where(slot == target_ref[...], 1.0, 0.0)
    own_copy.wait()
    core_copy.wait()
    relays = []

    def relay(c):
        far_copies[c].wait()
        copy = remote(
            place(far, chunks[c]), place(far, chunks[c]), relay_send.at[c], relay_recv.at[c],
            "band", partner,
        )
        copy.start()
        relays.append(copy)

    sends = []
    relay(0)
    for c, rows in enumerate(chunks):
        if c + 1 < CHUNKS:
            relay(c + 1)
        relays[c].wait()
        for i in range(each):
            level = c * each + i
            parts[me, level : level + 1] = jnp.sum(
                all_ref[level].astype(jnp.float32) * mixed[level], axis=0, keepdims=True
            )
        sends += spread_part(parts, part_send, part_recv, c, rows, nband)
    for copy in sends:
        copy.wait()
    total = parts[0]
    for band in range(1, nband):
        total = total + parts[band]
    increment = (scale * total).astype(jnp.bfloat16)

    spread[...] = lax.dot_general(
        select[...], increment, (((1,), (1,)), ((), ())), preferred_element_type=jnp.float32
    )
    for copy in loads:
        copy.wait()

    def project(j, carry):
        rows = pl.ds(pl.multiple_of(j * patch, patch), patch)
        value = spread[rows]
        total = jnp.zeros((patch, quarter), jnp.float32)
        for level in range(levels):
            total += value[:, level : level + 1] * interp[
                j, level * patch : (level + 1) * patch
            ].astype(jnp.float32)
        image[pl.ds(j, 1)] = jnp.sum(total, axis=0, keepdims=True)
        return carry

    lax.fori_loop(0, blocks, project, 0, unroll=2)
    send[...] = jnp.dot(
        placing, image[...], precision=lax.Precision.HIGHEST, preferred_element_type=jnp.float32
    ).reshape(send.shape)
    outs, backs = [], []
    for step in range(1, tiles):
        peer = lax.rem(tile + step, tiles)
        copy = remote(
            send.at[peer], arrived.at[tile], out_send.at[step - 1], out_recv.at[step - 1],
            "mem", peer,
        )
        copy.start()
        outs.append(copy)
    row = lax.broadcasted_iota(jnp.int32, (capacity, quarter), 0)

    def depart(source, value):
        rows = pl.ds(pl.multiple_of(source * capacity, capacity), capacity)
        live = jnp.where(row < counts_ref[source], 1.0, 0.0)
        result = live * obs[0, rows] * (innov[0, rows] - value)
        dep_ref[0, rows] = result
        return result.astype(jnp.bfloat16)

    back_own[...] = depart(tile, send[tile])
    for step in range(1, tiles):
        source = lax.rem(tile + tiles - step, tiles)
        outs[step - 1].wait_recv()
        rounded[source] = depart(source, arrived[source])
        copy = remote(
            rounded.at[source], back.at[tile], back_send.at[step - 1], back_recv.at[step - 1],
            "mem", source,
        )
        copy.start()
        backs.append(copy)
    back[tile] = back_own[...]
    for copy in outs:
        copy.wait_send()
    for copy in backs:
        copy.wait()
    image[...] = lax.dot_general(
        placing.astype(jnp.bfloat16), back[...].reshape(tiles * capacity, quarter),
        (((0,), (0,)), ((), ())), preferred_element_type=jnp.float32,
    )
    lane = lax.broadcasted_iota(jnp.int32, (patch, levels), 1)

    def gather_up(j, carry):
        own = jnp.broadcast_to(image[pl.ds(j, 1)], (levels, quarter)).astype(jnp.bfloat16)
        value = lax.dot_general(
            interp[j], own, (((1,), (1,)), ((), ())), preferred_element_type=jnp.float32
        )
        total = jnp.zeros((patch, levels), jnp.float32)
        for level in range(levels):
            total = jnp.where(lane == level, value[level * patch : (level + 1) * patch], total)
        spread[pl.ds(pl.multiple_of(j * patch, patch), patch)] = total
        return carry

    lax.fori_loop(0, blocks, gather_up, 0, unroll=4)
    high, low = split(spread[...])
    over = (((0,), (0,)), ((), ()))
    adj_parts[me] = lax.dot_general(
        high, select[...], over, preferred_element_type=jnp.float32
    ) + lax.dot_general(low, select[...], over, preferred_element_type=jnp.float32)
    sends = []
    for c, rows in enumerate(chunks):
        sends.append(spread_part(adj_parts, adj_send, adj_recv, c, rows, nband))
    local[...] = jnp.zeros_like(local)
    total = None
    for c in range(CHUNKS):
        for copy in sends[c]:
            copy.wait()
        for i in range(each):
            level = c * each + i
            adjoint = adj_parts[0, level : level + 1]
            for b in range(1, nband):
                adjoint = adjoint + adj_parts[b, level : level + 1]
            weighted = (all_ref[level].astype(jnp.float32) * adjoint).astype(jnp.bfloat16)
            term = lax.dot_general(
                weighted, eig_ref[level], (((1,), (1,)), ((), ())),
                preferred_element_type=jnp.float32,
            )
            total = term if total is None else total + term
    for b in range(nband):
        local[b, :, :modes_dev] = total[b * mem_dev : (b + 1) * mem_dev]
    copies = []
    for step in range(1, nband):
        peer = lax.rem(me + step, nband)
        copy = remote(
            local.at[peer], turned.at[me], turn_send.at[step - 1], turn_recv.at[step - 1],
            "band", peer,
        )
        copy.start()
        copies.append(copy)
    turned[me] = local[me]
    for copy in copies:
        copy.wait()
    own = turned[0]
    for b in range(1, nband):
        own = own + pltpu.roll(turned[b], b * modes_dev, 1)
    sums[tile] = own
    copies = []
    for step in range(1, tiles):
        peer = lax.rem(tile + step, tiles)
        copy = remote(
            sums.at[tile], sums.at[tile], sum_send.at[step - 1], sum_recv.at[step - 1],
            "mem", peer,
        )
        copy.start()
        copies.append(copy)
    for copy in copies:
        copy.wait()
    whole = sums[0]
    for t in range(1, tiles):
        whole = whole + sums[t]
    grad_ref[...] = control_ref[...] - scale * whole[:, : grad_ref.shape[1]]


def dma(*shape):
    return pltpu.SemaphoreType.DMA(shape)


def per_device(members, eigvecs, control, columns, interpolation, owners, innovation, obs_weight):
    nband = lax.axis_size("band")
    tiles = lax.axis_size("mem")
    band_idx = lax.axis_index("band")
    tile_idx = lax.axis_index("mem")
    mem_dev, levels, tile_cols = members.shape
    own_modes = eigvecs.shape[0]
    blocks, patch = columns.shape
    obs_block = interpolation.shape[2]
    capacity = innovation.shape[1] // tiles
    modes, total_members = control.shape
    scale = 1.0 / math.sqrt(modes * total_members)
    quarter = obs_block // nband
    eig_t = jnp.transpose(eigvecs, (1, 0, 2))
    mem_t = jnp.transpose(members, (1, 0, 2))
    weights = lax.dynamic_slice_in_dim(control, band_idx * own_modes, own_modes, 0)
    weights = weights.astype(jnp.bfloat16).T
    local_owner = lax.dynamic_slice_in_dim(owners, tile_idx * blocks, blocks, 0)
    order = jnp.arange(blocks, dtype=jnp.int32)
    earlier = order[None, :] < order[:, None]
    same = local_owner[:, None] == local_owner[None, :]
    rank = jnp.sum(jnp.logical_and(same, earlier), axis=1)
    target = (local_owner * capacity + rank)[None, :]
    counts = jnp.sum(owners.reshape(tiles, blocks) == tile_idx, axis=1)
    counts = jnp.broadcast_to(counts[:, None, None], (tiles, 1, quarter))
    own_control = lax.dynamic_slice_in_dim(control, band_idx * mem_dev, mem_dev, 1)
    lanes = pl.cdiv(modes, 128) * 128
    slots = (tiles, capacity, quarter)
    own_slots = (1, tiles * capacity, quarter)
    hbm = pl.BlockSpec(memory_space=pltpu.HBM)
    f32, bf16 = jnp.float32, jnp.bfloat16
    gradient, departure = pl.pallas_call(
        functools.partial(whole_kernel, nband, tiles, scale),
        out_shape=(
            jax.ShapeDtypeStruct((mem_dev, modes), f32),
            jax.ShapeDtypeStruct(own_slots, f32),
        ),
        in_specs=[VMEM] * 7 + [hbm] * 3,
        out_specs=(VMEM, VMEM),
        scratch_shapes=[
            pltpu.VMEM((levels, total_members, tile_cols), bf16),
            pltpu.VMEM((levels, total_members, tile_cols), f32),
            pltpu.VMEM((nband, levels, tile_cols), f32),
            pltpu.VMEM((nband, levels, tile_cols), f32),
            pltpu.VMEM((blocks * patch, tile_cols), bf16),
            pltpu.VMEM((blocks, levels * patch, quarter), bf16),
            pltpu.VMEM(own_slots, f32),
            pltpu.VMEM(own_slots, f32),
            pltpu.VMEM((blocks, quarter), f32),
            pltpu.VMEM((blocks * patch, levels), f32),
            pltpu.VMEM(slots, f32),
            pltpu.VMEM(slots, f32),
            pltpu.VMEM(slots, bf16),
            pltpu.VMEM(slots, bf16),
            pltpu.VMEM((capacity, quarter), bf16),
            pltpu.VMEM((nband, mem_dev, lanes), f32),
            pltpu.VMEM((nband, mem_dev, lanes), f32),
            pltpu.VMEM((tiles, mem_dev, lanes), f32),
            dma(4), dma(), dma(), dma(CHUNKS), dma(CHUNKS), dma(CHUNKS), dma(CHUNKS),
            dma(CHUNKS, nband - 1), dma(CHUNKS, nband - 1),
            dma(tiles - 1), dma(tiles - 1), dma(tiles - 1), dma(tiles - 1),
            dma(CHUNKS, nband - 1), dma(CHUNKS, nband - 1),
            dma(nband - 1), dma(nband - 1), dma(tiles - 1), dma(tiles - 1),
        ],
        compiler_params=pltpu.CompilerParams(
            collective_id=1, has_side_effects=True, vmem_limit_bytes=40 << 20
        ),
    )(
        mem_t, eig_t, weights, columns.T, target, counts, own_control.T,
        interpolation, innovation, obs_weight,
    )
    return (gradient.T, departure)


def solution(mesh):
    return jax.shard_map(
        per_device,
        mesh=mesh,
        in_specs=(
            P("band", None, "mem"),
            P("band", None, "mem"),
            P(),
            P("mem", None),
            P("mem", None, None),
            P(),
            P("mem", None, None),
            P("mem", None, None),
        ),
        out_specs=(P(None, "band"), P("mem", None, "band")),
        check_vma=False,
    )
```

time: 71.4 us -> 65.7 us (0.920)
  matrix products: 9 us -> 0 us
  Pallas kernels: 49.1 us -> 54.8 us
  local copies, waits for them, and re-layouts: 10.6 us -> 8.06 us
    dot_general x6 -> x0, matrix products: 9 us -> none  [the longest x1 3.4 us: per_device(): jnp.einsum('jro,jo->jr', interp, own_back, preferred_element_type=jnp.flo...]
    pallas_call x3 -> x1, Pallas kernels: 49.1 us -> 54.8 us  [per_device(): pl.pallas_call(functools.partial(whole_kernel, nband, tiles, scale), out_...]
    dynamic_slice x1 -> x0, local copies, waits for them, and re-layouts: 1.65 us -> none  [per_device(): lax.dynamic_slice_in_dim(obs_weight[0], band_idx * quarter, quarter, 1)]
    reshape x3 -> x0, local copies, waits for them, and re-layouts: 1.65 us -> none  [the longest x1 1.31 us: per_device(): jnp.transpose(spread.reshape(blocks, levels, patch), (1, 0, 2))]
    unnamed x15 -> x12, local copies, waits for them, and re-layouts: 5.77 us -> 7.07 us
    transpose x3 -> x1, local copies, waits for them, and re-layouts: 1.14 us -> 0.01 us  [per_device(): gradient, departure = pl.pallas_call(functools.partial(whole_kernel, nban...]
    mul x1 -> x0, other arithmetic: 1 us -> none  [per_device(): live_weight = live[:, :, None] * weight_part.reshape(slots)]
    broadcast_in_dim x0 -> x1, other arithmetic: none -> 0.77 us  [per_device(): target = (local_owner * capacity + rank)[None, :]]
where the time goes in v3:
time: 65.7 us; the launch traced here: 65.2 us
  Pallas kernels  54.8 us (83%)
  local copies, waits for them, and re-layouts  8.06 us (12%)
  other arithmetic  1.75 us (3%)
  between operations  0.68 us (1%)
    pallas_call x1, Pallas kernels, per_device(): pl.pallas_call(functools.partial(whole_kernel, nband, tiles, scale), out_...  54.8 us
    unnamed x12, local copies, waits for them, and re-layouts  7.07 us

profile of v3, /device:TPU:0, one launch (start us, length us, event | category | flops | bytes accessed | tf_op | source)
XLA Modules:
  0.0 65.2 jit_solution(7253746409334584510)
XLA Ops:
  0.6 0.0 copy-start
  0.7 0.8 %dynamic_slice.10 = s32[64]{0:T(128)S(1)} dynamic-slice(s32[512]{0:T(512)} %param.13, s32[]{:T(128)S(6)} %select_n.10), dynamic_slice_sizes={64} | dynamic-slice | bytes 516 | tf_op jit(solution)/shard_map/dynamic_slice | solution.py:299
  1.4 0.2 convert_reduce_fusion
  1.6 0.8 %add_bitcast_fusion.target_ref = s32[1,64]{1,0:T(1,128)S(1)} fusion(s32[64]{0:T(128)S(1)} %convert_reduce_fusion, s32[512]{0:T(512)} %param.13, s32[]{:T(128)S(6)} %select_n.10), kind=kLoop, calls=%fused_computation.9 | loop fusion | flops 128 | bytes 772 | tf_op jit(solution)/shard_map/broadcast_in_dim | solution.py:304
  2.4 0.7 %compare_convert_fusion = s32[512]{0:T(512)S(1)} fusion(s32[512]{0:T(512)} %param.13, s32[]{:T(128)S(6)} %axis_index.25), kind=kLoop, calls=%fused_computation.8 | loop fusion | flops 1024 | bytes 4100 | tf_op jit(solution)/shard_map/convert_element_type | solution.py:305
  3.0 0.1 reshape.14
  3.1 0.1 reduce_sum.19
  3.2 0.1 broadcast_in_dim.5.counts_ref
  3.3 0.0 copy-done
  3.3 0.1 fusion.1.weight_ref
  3.4 1.3 %copy.17 = bf16[16,16,1024]{2,0,1:T(8,128)(2,1)S(1)} copy(bf16[16,16,1024]{2,1,0:T(8,128)(2,1)} %param.8) | data formatting | bytes 1048576 | tf_op args[0]
  4.7 1.7 %copy.16 = bf16[28,16,1024]{2,0,1:T(8,128)(2,1)S(1)} copy(bf16[28,16,1024]{2,1,0:T(8,128)(2,1)} %param.9) | data formatting | bytes 1835008 | tf_op args[1]
  6.4 0.0 copy-start.1
  6.4 1.0 %copy-done.1 = f32[1,256,512]{2,1,0:T(8,128)S(1)} copy-done((f32[1,256,512]{2,1,0:T(8,128)S(1)}, f32[1,256,512]{2,1,0:T(8,128)}, u32[]{:S(2)}) %copy-start.1) | copy-done | bytes 524312
  7.5 0.0 copy-start.2
  7.5 1.0 %copy-done.2 = f32[1,256,512]{2,1,0:T(8,128)S(1)} copy-done((f32[1,256,512]{2,1,0:T(8,128)S(1)}, f32[1,256,512]{2,1,0:T(8,128)}, u32[]{:S(2)}) %copy-start.2) | copy-done | bytes 524312
  8.5 0.0 copy-start.3
  8.5 0.7 %copy-done.3 = s32[64,16]{0,1:T(8,128)S(1)} copy-done((s32[64,16]{0,1:T(8,128)S(1)}, s32[64,16]{0,1:T(8,128)}, u32[]{:S(2)}) %copy-start.3) | copy-done | bytes 4120
  9.2 54.8 %shard_map.95 = (f32[16,112]{1,0:T(8,128)S(1)}, f32[1,256,128]{2,1,0:T(8,128)S(1)}) custom-call(bf16[16,16,1024]{2,1,0:T(8,128)(2,1)S(1)} %bitcast.15, bf16[16,28,1024]{2,1,0:T(8,128)(2,1)S(1)} %bitcast.14, bf16[64,28]{1,0:T(8,128)(2,1)S(1)} %fusion.1.weight_ref, s32[16,64]{1,0:T(8,128)S(1)} %bitcast.16, s32[1,64]{1,0:T(1,128)S(1)} %add_bitcast_fusion.target_ref, ...), custom_call_target="tpu_custom_call" | custom-call | tf_op jit(solution)/shard_map/pallas_call | solution.py:313
  64.0 0.6 copy.20
  64.6 0.7 %copy.21 = f32[1,256,128]{2,1,0:T(8,128)} copy(f32[1,256,128]{2,1,0:T(8,128)S(1)} %get-tuple-element.9) | data formatting | bytes 262144
  (1 shorter events, 0.0 us)
Async XLA Ops:
  0.6 2.7 %copy-start = (f32[112,64]{0,1:T(8,128)S(1)}, f32[112,64]{0,1:T(8,128)}, u32[]{:S(2)}) copy-start(f32[112,64]{0,1:T(8,128)} %param.10) | copy-start | bytes 86020
  6.4 1.0 %copy-start.1 = (f32[1,256,512]{2,1,0:T(8,128)S(1)}, f32[1,256,512]{2,1,0:T(8,128)}, u32[]{:S(2)}) copy-start(f32[1,256,512]{2,1,0:T(8,128)} %innov_hbm.1) | copy-start | bytes 1572868
  7.5 1.0 %copy-start.2 = (f32[1,256,512]{2,1,0:T(8,128)S(1)}, f32[1,256,512]{2,1,0:T(8,128)}, u32[]{:S(2)}) copy-start(f32[1,256,512]{2,1,0:T(8,128)} %obs_hbm.1) | copy-start | bytes 1572868
  8.5 0.7 %copy-start.3 = (s32[64,16]{0,1:T(8,128)S(1)}, s32[64,16]{0,1:T(8,128)}, u32[]{:S(2)}) copy-start(s32[64,16]{0,1:T(8,128)} %param.11) | copy-start | bytes 12292

commit v4 on v3

--- a/solution.py
+++ b/solution.py
@@ -53,7 +53,7 @@
 
 
 def whole_kernel(
-    nband, tiles, scale, mem_ref, eig_ref, weight_ref, cols_ref, target_ref, counts_ref,
+    nband, tiles, scale, mem_ref, eig_ref, weight_ref, cols_ref, owners_ref,
     control_ref, interp_hbm, innov_hbm, obs_hbm, grad_ref, dep_ref,
     all_ref, mixed, parts, adj_parts, select, interp, innov, obs, image, spread, send, arrived,
     rounded, back, back_own, local, turned, sums,
@@ -109,8 +109,24 @@
         select[j * patch : (j + 1) * patch] = jnp.where(
             cols_ref[:, j : j + 1] == column, 1.0, 0.0
         ).astype(jnp.bfloat16)
+    owner = owners_ref[pl.ds(tile, 1)].astype(jnp.float32)
+    down = lax.broadcasted_iota(jnp.int32, (blocks, blocks), 0)
+    across = lax.broadcasted_iota(jnp.int32, (blocks, blocks), 1)
+    owner_column = jnp.sum(jnp.where(down == across, owner, 0.0), axis=1, keepdims=True)
+    same = jnp.where(jnp.logical_and(owner_column == owner, down < across), 1.0, 0.0)
+    rank = jnp.sum(same, axis=0, keepdims=True)
+    target = (owner * capacity + rank).astype(jnp.int32)
     slot = lax.broadcasted_iota(jnp.int32, (tiles * capacity, blocks), 0)
-    placing = jnp.where(slot == target_ref[...], 1.0, 0.0)
+    placing = jnp.where(slot == target, 1.0, 0.0)
+    counts = jnp.sum(
+        jnp.where(owners_ref[...] == tile, 1.0, 0.0), axis=1, keepdims=True
+    ).astype(jnp.int32)
+    for copy in loads:
+        copy.wait()
+    row = lax.broadcasted_iota(jnp.int32, (capacity, quarter), 0)
+    for t in range(tiles):
+        rows = slice(t * capacity, (t + 1) * capacity)
+        obs[0, rows] = jnp.where(row < counts[t : t + 1], 1.0, 0.0) * obs[0, rows]
     own_copy.wait()
     core_copy.wait()
     relays = []
@@ -146,8 +162,6 @@
     spread[...] = lax.dot_general(
         select[...], increment, (((1,), (1,)), ((), ())), preferred_element_type=jnp.float32
     )
-    for copy in loads:
-        copy.wait()
 
     def project(j, carry):
         rows = pl.ds(pl.multiple_of(j * patch, patch), patch)
@@ -160,7 +174,7 @@
         image[pl.ds(j, 1)] = jnp.sum(total, axis=0, keepdims=True)
         return carry
 
-    lax.fori_loop(0, blocks, project, 0, unroll=2)
+    lax.fori_loop(0, blocks, project, 0, unroll=4)
     send[...] = jnp.dot(
         placing, image[...], precision=lax.Precision.HIGHEST, preferred_element_type=jnp.float32
     ).reshape(send.shape)
@@ -173,12 +187,10 @@
         )
         copy.start()
         outs.append(copy)
-    row = lax.broadcasted_iota(jnp.int32, (capacity, quarter), 0)
 
     def depart(source, value):
         rows = pl.ds(pl.multiple_of(source * capacity, capacity), capacity)
-        live = jnp.where(row < counts_ref[source], 1.0, 0.0)
-        result = live * obs[0, rows] * (innov[0, rows] - value)
+        result = obs[0, rows] * (innov[0, rows] - value)
         dep_ref[0, rows] = result
         return result.astype(jnp.bfloat16)
 
@@ -296,14 +308,6 @@
     mem_t = jnp.transpose(members, (1, 0, 2))
     weights = lax.dynamic_slice_in_dim(control, band_idx * own_modes, own_modes, 0)
     weights = weights.astype(jnp.bfloat16).T
-    local_owner = lax.dynamic_slice_in_dim(owners, tile_idx * blocks, blocks, 0)
-    order = jnp.arange(blocks, dtype=jnp.int32)
-    earlier = order[None, :] < order[:, None]
-    same = local_owner[:, None] == local_owner[None, :]
-    rank = jnp.sum(jnp.logical_and(same, earlier), axis=1)
-    target = (local_owner * capacity + rank)[None, :]
-    counts = jnp.sum(owners.reshape(tiles, blocks) == tile_idx, axis=1)
-    counts = jnp.broadcast_to(counts[:, None, None], (tiles, 1, quarter))
     own_control = lax.dynamic_slice_in_dim(control, band_idx * mem_dev, mem_dev, 1)
     lanes = pl.cdiv(modes, 128) * 128
     slots = (tiles, capacity, quarter)
@@ -316,7 +320,7 @@
             jax.ShapeDtypeStruct((mem_dev, modes), f32),
             jax.ShapeDtypeStruct(own_slots, f32),
         ),
-        in_specs=[VMEM] * 7 + [hbm] * 3,
+        in_specs=[VMEM] * 6 + [hbm] * 3,
         out_specs=(VMEM, VMEM),
         scratch_shapes=[
             pltpu.VMEM((levels, total_members, tile_cols), bf16),
@@ -347,8 +351,8 @@
             collective_id=1, has_side_effects=True, vmem_limit_bytes=40 << 20
         ),
     )(
-        mem_t, eig_t, weights, columns.T, target, counts, own_control.T,
-        interpolation, innovation, obs_weight,
+        mem_t, eig_t, weights, columns.T, owners.reshape(tiles, blocks), own_control.T,
+        *[pltpu.with_memory_space_constraint(x, pltpu.HBM) for x in (interpolation, innovation, obs_weight)],
     )
     return (gradient.T, departure)
 

time: 65.7 us -> 60.4 us (0.919)
  local copies, waits for them, and re-layouts: 8.06 us -> 5.82 us
  other arithmetic: 1.75 us -> 0 us
  Pallas kernels: 54.8 us -> 53.6 us
    unnamed x12 -> x8, local copies, waits for them, and re-layouts: 7.07 us -> 4.98 us
    pallas_call x1, Pallas kernels: 54.8 us -> 53.6 us  [per_device(): pl.pallas_call(functools.partial(whole_kernel, nband, tiles, scale), out_...]
    broadcast_in_dim x1 -> x0, other arithmetic: 0.77 us -> none  [per_device(): target = (local_owner * capacity + rank)[None, :]]
    dynamic_slice x1 -> x0, local copies, waits for them, and re-layouts: 0.76 us -> none  [per_device(): local_owner = lax.dynamic_slice_in_dim(owners, tile_idx * blocks, blocks, 0)]
    reshape x0 -> x1, local copies, waits for them, and re-layouts: none -> 0.76 us  [per_device(): owners.reshape(tiles, blocks)]
    convert_element_type x1 -> x0, other arithmetic: 0.68 us -> none  [per_device(): counts = jnp.sum(owners.reshape(tiles, blocks) == tile_idx, axis=1)]
where the time goes in v4:
time: 60.4 us; the launch traced here: 60.1 us
  Pallas kernels  53.6 us (89%)
  local copies, waits for them, and re-layouts  5.82 us (10%)
  between operations  0.67 us (1%)
    pallas_call x1, Pallas kernels, per_device(): pl.pallas_call(functools.partial(whole_kernel, nband, tiles, scale), out_...  53.6 us
    unnamed x8, local copies, waits for them, and re-layouts  4.98 us

profile of v4, /device:TPU:0, one launch (start us, length us, event | category | flops | bytes accessed | tf_op | source)
XLA Modules:
  0.0 60.1 jit_solution(5286740254392866444)
XLA Ops:
  0.6 0.0 copy-start
  0.7 0.8 %reshape.7.owners_ref = s32[8,64]{1,0:T(8,128)S(1)} reshape(s32[512]{0:T(512)} %param.13) | data formatting | bytes 4096 | tf_op jit(solution)/shard_map/reshape | solution.py:354
  1.4 0.0 copy-done
  1.4 0.1 fusion.weight_ref
  1.5 1.3 %copy.15 = bf16[16,16,1024]{2,0,1:T(8,128)(2,1)S(1)} copy(bf16[16,16,1024]{2,1,0:T(8,128)(2,1)} %param.8) | data formatting | bytes 1048576 | tf_op args[0]
  2.8 1.7 %copy.14 = bf16[28,16,1024]{2,0,1:T(8,128)(2,1)S(1)} copy(bf16[28,16,1024]{2,1,0:T(8,128)(2,1)} %param.9) | data formatting | bytes 1835008 | tf_op args[1]
  4.5 0.0 copy-start.1
  4.5 0.7 %copy-done.1 = s32[64,16]{0,1:T(8,128)S(1)} copy-done((s32[64,16]{0,1:T(8,128)S(1)}, s32[64,16]{0,1:T(8,128)}, u32[]{:S(2)}) %copy-start.1) | copy-done | bytes 4120
  5.2 53.6 %shard_map.95 = (f32[16,112]{1,0:T(8,128)S(1)}, f32[1,256,128]{2,1,0:T(8,128)S(1)}) custom-call(bf16[16,16,1024]{2,1,0:T(8,128)(2,1)S(1)} %bitcast.13, bf16[16,28,1024]{2,1,0:T(8,128)(2,1)S(1)} %bitcast.12, bf16[64,28]{1,0:T(8,128)(2,1)S(1)} %fusion.weight_ref, s32[16,64]{1,0:T(8,128)S(1)} %bitcast.14, s32[8,64]{1,0:T(8,128)S(1)} %reshape.7.owners_ref, ...), custom_call_target="tpu_custom_call" | custom-call | tf_op jit(solution)/shard_map/pallas_call | solution.py:317
  58.8 0.6 %copy.18 = f32[112,16]{0,1:T(8,128)} copy(f32[112,16]{0,1:T(8,128)S(1)} %bitcast.15) | data formatting | bytes 14336
  59.4 0.7 %copy.19 = f32[1,256,128]{2,1,0:T(8,128)} copy(f32[1,256,128]{2,1,0:T(8,128)S(1)} %get-tuple-element.9) | data formatting | bytes 262144
  (1 shorter events, 0.0 us)
Async XLA Ops:
  0.6 0.8 %copy-start = (f32[112,64]{0,1:T(8,128)S(1)}, f32[112,64]{0,1:T(8,128)}, u32[]{:S(2)}) copy-start(f32[112,64]{0,1:T(8,128)} %param.10) | copy-start | bytes 86020
  4.5 0.7 %copy-start.1 = (s32[64,16]{0,1:T(8,128)S(1)}, s32[64,16]{0,1:T(8,128)}, u32[]{:S(2)}) copy-start(s32[64,16]{0,1:T(8,128)} %param.11) | copy-start | bytes 12292
